TPU v7x, 32 devices: a whole 2x2x4 slice. The times are simulated.
32 devices in a mesh: vocab: 8 (over z, x), batch: 4 (over y, core).
Axes of the slice: x: 2, y: 2, z: 4, core: 2. Of those that a mesh axis runs over, the one named last changes fastest.
Arguments:
- hidden: bfloat16 [256, 1024], P(('vocab', 'batch'))
- embedding: bfloat16 [8192, 1024], P('vocab')
- block_counts: int32 [64], P('vocab'), may hold values from 1 to 4095
- lang_blocks: int32 [200, 64], replicated, may hold values from -1 to 63, as said below
- sent_lang: int32 [4], replicated, may hold values from 0 to 199
- targets: int32 [256], replicated, may hold values from 0 to 8191, as said below
Outputs:
- token_loss: float32 [256], P(('vocab', 'batch'))
- grad_embed: bfloat16 [8192, 1024], P(('vocab', 'batch'))
Inputs may be any that keep to these rules, and one draw needn't show every extreme that they name: `lang_blocks`: each list holds distinct block numbers and then -1 padding; the first entry of every list is block 0; at least 16 entries are blocks, and some language fills all 64 entries. `targets`: the target of token t lies in a block listed for the language of sentence t // 64.
All inputs are finite; a program needn't handle non-finite values.
Results may differ from a plain program's by a relative error of at most 0.0075.
Values may be sent and summed in bfloat16 or wider, within the bound.
No kernel may reach another device: no remote copies, remote signals or barrier semaphores. Data moves between devices by JAX's collectives and lax.ppermute only.
A program may use at most 64 MiB of HBM per device.

v0:
```python
import functools

import jax
import jax.numpy as jnp
from jax import lax
from jax.experimental import pallas as pl
from jax.experimental.pallas import tpu as pltpu
from jax.sharding import PartitionSpec as P


SEQ = 64
LANES = 128
KERNEL_VMEM = 8 * 1024 * 1024


masked_fill = float(jnp.finfo(jnp.float32).min)


def centre_first(count):
    return sorted(range(count), key=lambda i: (abs(2 * (i // 2) - count // 2 + 1), -(i % 2), i))


def iota(shape, axis):
    return lax.broadcasted_iota(jnp.int32, shape, axis)


def contract_last(a, b):
    return lax.dot_general(a, b, (((1,), (1,)), ((), ())), preferred_element_type=jnp.float32)


def prepare_kernel(
    order, tok_dev, batch_count, sent_hbm, count_hbm, lists_hbm, targets_hbm, emb_hbm,
    bias_ref, target_ref, kept_ref, sent_ref, count_ref, lists_ref, targets_ref, sems,
):
    sources = (sent_hbm, count_hbm, lists_hbm, targets_hbm, emb_hbm)
    places = (sent_ref, count_ref, lists_ref, targets_ref, kept_ref)
    fetches = [
        pltpu.make_async_copy(src, dst, sems.at[i])
        for i, (src, dst) in enumerate(zip(sources, places))
    ]
    for fetch in fetches:
        fetch.start()
    vocab_index = lax.axis_index("vocab")
    batch_index = lax.axis_index("batch")
    local_blocks, tokens = bias_ref.shape
    group_tokens = tokens // batch_count
    languages = lists_ref.shape[1]

    lane = iota((1, tokens), 1)
    source = batch_index ^ (lane // group_tokens)
    position = (lane % group_tokens) // tok_dev
    place = jnp.zeros((1, tokens), jnp.int32)
    for j, v in enumerate(order):
        place = jnp.where(position == j, v, place)
    token = (place * batch_count + source) * tok_dev + lane % tok_dev
    sentence = token // SEQ

    for fetch in fetches[:-1]:
        fetch.wait()
    found = jnp.zeros((1, tokens), jnp.float32)
    for start in range(0, tokens, LANES):
        size = min(LANES, tokens - start)
        part = targets_ref[:, start : start + size].astype(jnp.float32)
        eye = iota((size, size), 0) == iota((size, size), 1)
        column = jnp.sum(jnp.where(eye, part, 0.0), axis=1, keepdims=True)
        hit = (iota((size, tokens), 0) + start) == token
        found = found + jnp.sum(jnp.where(hit, column, 0.0), axis=0, keepdims=True)
    target_ref[...] = found.astype(jnp.int32)

    block = iota((local_blocks, 1), 0)
    member = jnp.zeros((local_blocks, languages), jnp.float32)
    counts = jnp.zeros((local_blocks, 1), jnp.float32)
    for k in range(local_blocks):
        listed = jnp.where(lists_ref[...] == vocab_index * local_blocks + k, 1.0, 0.0)
        listed = jnp.max(listed, axis=0, keepdims=True)
        member = jnp.where(block == k, listed, member)
        counts = jnp.where(block == k, count_ref[k].astype(jnp.float32), counts)
    log_counts = jnp.log(counts)
    bias = jnp.full((local_blocks, tokens), jnp.inf, jnp.float32)
    language = iota((local_blocks, languages), 1)
    for s in range(sent_ref.shape[0]):
        picked = jnp.where(language == sent_ref[s], member, 0.0)
        picked = jnp.max(picked, axis=1, keepdims=True)
        bias = jnp.where((sentence == s) & (picked > 0.5), log_counts, bias)
    bias_ref[...] = bias
    fetches[-1].wait()


def stats_kernel(bias_ref, target_ref, emb_ref, rows_ref, stats_ref, logits_ref):
    vocab_index = lax.axis_index("vocab")
    group_tokens = rows_ref.shape[0]
    local_rows = emb_ref.shape[0]
    local_blocks = bias_ref.shape[0]
    block_width = local_rows // local_blocks

    raw = contract_last(emb_ref[...], rows_ref[...])
    own_target = target_ref[:, :group_tokens] - vocab_index * local_rows
    word = iota((block_width, group_tokens), 0)
    aimed = jnp.zeros((block_width, group_tokens), jnp.float32)
    peaks, totals = [], []
    for start in range(0, local_blocks, 2):
        top = None
        for k in range(start, start + 2):
            rows = slice(k * block_width, (k + 1) * block_width)
            cell = bias_ref[k : k + 1, :group_tokens]
            logits = jnp.where(cell < jnp.inf, raw[rows] - cell, -jnp.inf)
            logits_ref[rows, :] = logits
            top = logits if top is None else jnp.maximum(top, logits)
            aimed = jnp.where(word + k * block_width == own_target, logits, aimed)
        peaks.append(jnp.maximum(jnp.max(top, axis=0, keepdims=True), masked_fill))
        rows = slice(start * block_width, (start + 2) * block_width)
        part = jnp.exp(logits_ref[rows, :] - peaks[-1])
        totals.append(jnp.sum(part, axis=0, keepdims=True))
    peak = functools.reduce(jnp.maximum, peaks)
    total = sum(t * jnp.exp(p - peak) for p, t in zip(peaks, totals))
    aimed = jnp.sum(aimed, axis=0, keepdims=True)
    row = iota((2, group_tokens), 0)
    first = jnp.where(row == 0, peak, aimed)
    second = jnp.where(row == 0, total, 0.0)
    for p in range(stats_ref.shape[0]):
        stats_ref[p, :, :group_tokens] = first
        stats_ref[p, :, group_tokens:] = second


def scores_kernel(batch_count, bias_ref, target_ref, emb_ref, *refs):
    row_refs = refs[:batch_count]
    logits_ref, everyone_ref = refs[batch_count:]
    batch_index = lax.axis_index("batch")
    group_tokens = row_refs[0].shape[0]
    own_rows = logits_ref.shape[0]
    block_width = emb_ref.shape[0] // bias_ref.shape[0]
    own_blocks = own_rows // block_width

    for m in range(batch_count):
        everyone_ref[m * group_tokens : (m + 1) * group_tokens, :] = row_refs[m][...]
    mine = emb_ref[pl.ds(pl.multiple_of(batch_index * own_rows, own_rows), own_rows), :]
    raw = contract_last(mine, everyone_ref[...])
    for k in range(own_blocks):
        rows = slice(k * block_width, (k + 1) * block_width)
        cell = bias_ref[pl.ds(batch_index * own_blocks + k, 1), :]
        logits_ref[rows, :] = jnp.where(cell < jnp.inf, raw[rows] - cell, -jnp.inf)


def grad_kernel(
    order, tok_dev, batch_count, stats_ref, target_ref, logits_ref, everyone_ref,
    loss_ref, grad_ref, weight_ref, result_ref, mine_ref, sems,
):
    vocab_index = lax.axis_index("vocab")
    batch_index = lax.axis_index("batch")
    own_rows, tokens = logits_ref.shape
    group_tokens = tokens // batch_count
    width = everyone_ref.shape[1]
    vocab_count = stats_ref.shape[0] // batch_count

    rows = []
    for m in range(batch_count):
        group = batch_index ^ m
        parts = stats_ref[pl.ds(group, vocab_count, stride=batch_count), 0, :]
        peak = jnp.max(parts, axis=0, keepdims=True)
        totals = pltpu.roll(parts, group_tokens, 1)
        total = jnp.sum(totals * jnp.exp(parts - peak), axis=0, keepdims=True)
        log_total = peak + jnp.log(total)
        if m == 0:
            aimed = stats_ref[pl.ds(group, vocab_count, stride=batch_count), 1, :]
            loss = log_total - jnp.sum(aimed, axis=0, keepdims=True)
            my_place = jnp.int32(0)
            for j, v in enumerate(order):
                my_place = jnp.where(vocab_index == v, j, my_place)
            wanted = my_place * tok_dev + iota((tok_dev, LANES), 0)
            chosen = jnp.where(iota((tok_dev, LANES), 1) == wanted, loss, 0.0)
            chosen = jnp.sum(chosen, axis=1, keepdims=True)
            eye = iota((tok_dev, tok_dev), 0) == iota((tok_dev, tok_dev), 1)
            mine_ref[...] = jnp.sum(jnp.where(eye, chosen, 0.0), axis=0, keepdims=True)
            pushes = [pltpu.make_async_copy(mine_ref, loss_ref, sems.at[0])]
            pushes[0].start()
        rows.append(log_total)
    low = iota((1, LANES), 1) < group_tokens
    pairs = [
        jnp.where(low, rows[m], pltpu.roll(rows[m + 1], group_tokens, 1))
        for m in range(0, batch_count, 2)
    ]
    target = target_ref[...] - (vocab_index * batch_count + batch_index) * own_rows
    for i, pair in enumerate(pairs):
        lanes = slice(i * LANES, (i + 1) * LANES)
        weight = jnp.exp(logits_ref[:, lanes] - pair)
        hit = iota((own_rows, LANES), 0) == target[:, lanes]
        weight_ref[:, lanes] = (weight - jnp.where(hit, 1.0, 0.0)).astype(jnp.bfloat16)
    chunks = sems.shape[0] - 1
    chunk = width // chunks
    for c in range(chunks):
        columns = slice(c * chunk, (c + 1) * chunk)
        result_ref[:, columns] = jnp.dot(
            weight_ref[...], everyone_ref[:, columns], preferred_element_type=jnp.float32
        ).astype(result_ref.dtype)
        push = pltpu.make_async_copy(
            result_ref.at[:, columns], grad_ref.at[:, columns], sems.at[c + 1]
        )
        push.start()
        pushes.append(push)
    for push in pushes:
        push.wait()


VMEM = pl.BlockSpec(memory_space=pltpu.VMEM)


def fused_body(hidden, embedding, block_counts, lang_blocks, sent_lang, targets):
    tok_dev, width = hidden.shape
    vocab_count = lax.axis_size("vocab")
    batch_count = lax.axis_size("batch")
    local_rows = embedding.shape[0]
    local_blocks = block_counts.shape[0]
    own_rows = local_rows // batch_count
    group_tokens = vocab_count * tok_dev
    tokens = group_tokens * batch_count
    devices = vocab_count * batch_count
    order = centre_first(vocab_count)
    both = ("vocab", "batch")
    groups = [[v * batch_count + b for v in order] for b in range(batch_count)]
    struct = jax.ShapeDtypeStruct

    copies = jnp.broadcast_to(hidden[None], (vocab_count, tok_dev, width))
    gathered = lax.all_to_all(copies, both, 0, 0, tiled=True, axis_index_groups=groups)
    gathered = gathered.reshape(group_tokens, width)
    limit = pltpu.CompilerParams(vmem_limit_bytes=KERNEL_VMEM)
    bias, target_ids, kept = pl.pallas_call(
        functools.partial(prepare_kernel, order, tok_dev, batch_count),
        out_shape=(
            struct((local_blocks, tokens), jnp.float32),
            struct((1, tokens), jnp.int32),
            struct(embedding.shape, embedding.dtype),
        ),
        in_specs=[pl.BlockSpec(memory_space=pltpu.HBM)] * 5,
        out_specs=(VMEM, VMEM, VMEM),
        scratch_shapes=[
            pltpu.SMEM(sent_lang.shape, jnp.int32),
            pltpu.SMEM(block_counts.shape, jnp.int32),
            pltpu.VMEM(lang_blocks.shape[::-1], jnp.int32),
            pltpu.VMEM((1, tokens), jnp.int32),
            pltpu.SemaphoreType.DMA((5,)),
        ],
        compiler_params=limit,
        name="prepare",
        cost_estimate=pl.CostEstimate(
            flops=tokens * tokens, bytes_accessed=4 * local_rows * width, transcendentals=0
        ),
    )(
        *(
            pltpu.with_memory_space_constraint(x, pltpu.HBM)
            for x in (sent_lang, block_counts, lang_blocks.T, targets.reshape(1, -1), embedding)
        )
    )
    stats = pl.pallas_call(
        stats_kernel,
        out_shape=struct((devices, 2, 2 * group_tokens), jnp.float32),
        in_specs=[VMEM] * 4,
        out_specs=VMEM,
        scratch_shapes=[pltpu.VMEM((local_rows, group_tokens), jnp.float32)],
        compiler_params=limit,
        name="stats",
        cost_estimate=pl.CostEstimate(
            flops=2 * local_rows * group_tokens * width,
            bytes_accessed=2 * local_rows * width,
            transcendentals=local_rows * group_tokens,
        ),
    )(bias, target_ids, kept, gathered)
    stats = lax.all_to_all(stats, both, 0, 0, tiled=True)
    pieces = [gathered]
    step = batch_count // 2
    while step:
        pairs = [(b, b ^ step) for b in range(batch_count)]
        received = [lax.ppermute(piece, "batch", pairs) for piece in pieces]
        pieces = [half for pair in zip(pieces, received) for half in pair]
        step //= 2
    logits, everyone = pl.pallas_call(
        functools.partial(scores_kernel, batch_count),
        out_shape=(
            struct((own_rows, tokens), jnp.float32),
            struct((tokens, width), jnp.bfloat16),
        ),
        in_specs=[VMEM] * (3 + batch_count),
        out_specs=(VMEM, VMEM),
        compiler_params=limit,
        name="scores",
        cost_estimate=pl.CostEstimate(
            flops=2 * own_rows * tokens * width,
            bytes_accessed=2 * own_rows * width,
            transcendentals=0,
        ),
    )(bias, target_ids, kept, *pieces)
    loss, grad = pl.pallas_call(
        functools.partial(grad_kernel, order, tok_dev, batch_count),
        out_shape=(struct((1, tok_dev), jnp.float32), struct((own_rows, width), jnp.bfloat16)),
        in_specs=[VMEM] * 4,
        out_specs=(pl.BlockSpec(memory_space=pl.ANY),) * 2,
        scratch_shapes=[
            pltpu.VMEM((own_rows, tokens), jnp.bfloat16),
            pltpu.VMEM((own_rows, width), jnp.bfloat16),
            pltpu.VMEM((1, tok_dev), jnp.float32),
            pltpu.SemaphoreType.DMA((5,)),
        ],
        compiler_params=limit,
        name="grad",
        cost_estimate=pl.CostEstimate(
            flops=2 * own_rows * tokens * width,
            bytes_accessed=2 * own_rows * width,
            transcendentals=own_rows * tokens,
        ),
    )(stats, target_ids, logits, everyone)
    return (loss.reshape(tok_dev), grad)


def body(hidden, embedding, block_counts, lang_blocks, sent_lang, targets):
    tok_dev, width = hidden.shape
    vocab_count = lax.axis_size("vocab")
    batch_count = lax.axis_size("batch")
    vocab_index = lax.axis_index("vocab")
    batch_index = lax.axis_index("batch")
    local_rows = embedding.shape[0]
    local_blocks = block_counts.shape[0]
    block_width = local_rows // local_blocks
    own_rows = local_rows // batch_count
    own_blocks = own_rows // block_width
    group_tokens = vocab_count * tok_dev
    order = centre_first(vocab_count)
    both = ("vocab", "batch")
    groups = [[v * batch_count + b for v in order] for b in range(batch_count)]

    copies = jnp.broadcast_to(hidden[None], (vocab_count, tok_dev, width))
    gathered = lax.all_to_all(copies, both, 0, 0, tiled=True, axis_index_groups=groups)
    gathered = gathered.reshape(group_tokens, width)
    pieces = [gathered]
    for step in range(1, batch_count):
        pairs = [(b, b ^ step) for b in range(batch_count)]
        pieces.append(lax.ppermute(gathered, "batch", pairs))
    everyone = jnp.concatenate(pieces, axis=0)

    sources = batch_index ^ jnp.arange(batch_count, dtype=jnp.int32)
    places = jnp.array(order, jnp.int32)
    token_ids = (
        (places[None, :, None] * batch_count + sources[:, None, None]) * tok_dev
        + jnp.arange(tok_dev, dtype=jnp.int32)[None, None, :]
    ).reshape(batch_count, group_tokens)
    target_table = targets.reshape(vocab_count, batch_count, tok_dev)
    target_table = jnp.stack([target_table[v] for v in order], axis=1)
    target_ids = jnp.stack(
        [
            lax.dynamic_index_in_dim(target_table, batch_index ^ step, 0, keepdims=False)
            for step in range(batch_count)
        ]
    ).reshape(batch_count, group_tokens)

    block_ids = vocab_index * local_blocks + jnp.arange(local_blocks, dtype=jnp.int32)
    sentence_lists = lang_blocks[sent_lang]
    member = jnp.any(sentence_lists[:, None, :] == block_ids[None, :, None], axis=2)
    sentence_ids = jnp.arange(sent_lang.shape[0], dtype=jnp.int32)
    sentence_hit = (token_ids // SEQ)[None] == sentence_ids[:, None, None]
    allowed = jnp.any(member[:, :, None, None] & sentence_hit[:, None], axis=0)
    log_sampling = jnp.log(block_counts.astype(jnp.float32))

    own_allowed = allowed[:, 0][:, None, :]
    logits = lax.dot_general(
        embedding, gathered, (((1,), (1,)), ((), ())), preferred_element_type=jnp.float32
    ).reshape(local_blocks, block_width, group_tokens) - log_sampling[:, None, None]
    word_ids = (vocab_index * local_rows + jnp.arange(local_rows, dtype=jnp.int32)).reshape(
        local_blocks, block_width
    )
    is_target = word_ids[:, :, None] == target_ids[0][None, None, :]
    local_peak = jnp.max(jnp.where(own_allowed, logits, masked_fill), axis=(0, 1))
    local_total = jnp.sum(
        jnp.where(own_allowed, jnp.exp(logits - local_peak[None, None, :]), 0.0), axis=(0, 1)
    )
    local_target = jnp.sum(jnp.where(is_target, logits, 0.0), axis=(0, 1))
    blank = jnp.zeros_like(local_peak)
    stats = jnp.stack([local_peak, local_total, local_target] + [blank] * 5)
    stats = jnp.broadcast_to(stats[None], (vocab_count * batch_count,) + stats.shape)
    stats = lax.all_to_all(stats, both, 0, 0, tiled=True)
    stats = stats.reshape(vocab_count, batch_count, 8, group_tokens)
    peak = jnp.max(stats[:, :, 0], axis=0)
    total = jnp.sum(stats[:, :, 1] * jnp.exp(stats[:, :, 0] - peak[None]), axis=0)
    log_total = peak + jnp.log(total)
    target_logit = jnp.sum(stats[:, :, 2], axis=0)
    every_loss = lax.dynamic_index_in_dim(log_total - target_logit, batch_index, 0, keepdims=False)
    my_place = jnp.sum(jnp.where(places == vocab_index, jnp.arange(vocab_count), 0))
    token_loss = lax.dynamic_slice_in_dim(every_loss, my_place * tok_dev, tok_dev, 0)
    ordered = jnp.stack(
        [
            lax.dynamic_index_in_dim(log_total, batch_index ^ step, 0, keepdims=False)
            for step in range(batch_count)
        ]
    ).reshape(-1)

    mine = lax.dynamic_slice_in_dim(embedding, batch_index * own_rows, own_rows, 0)
    my_blocks = batch_index * own_blocks
    my_sampling = lax.dynamic_slice_in_dim(log_sampling, my_blocks, own_blocks, 0)
    my_allowed = lax.dynamic_slice_in_dim(allowed, my_blocks, own_blocks, 0)
    my_allowed = my_allowed.reshape(own_blocks, 1, -1)
    my_words = lax.dynamic_slice_in_dim(word_ids, my_blocks, own_blocks, 0)
    my_logits = lax.dot_general(
        mine, everyone, (((1,), (1,)), ((), ())), preferred_element_type=jnp.float32
    ).reshape(own_blocks, block_width, -1) - my_sampling[:, None, None]
    weights = jnp.where(my_allowed, jnp.exp(my_logits - ordered[None, None, :]), 0.0)
    hits = my_words[:, :, None] == target_ids.reshape(-1)[None, None, :]
    grad_logits = (weights - hits.astype(jnp.float32)).astype(jnp.bfloat16)
    grad_embed = lax.dot_general(
        grad_logits.reshape(own_rows, -1),
        everyone,
        (((1,), (0,)), ((), ())),
        preferred_element_type=jnp.float32,
    ).astype(jnp.bfloat16)
    return (token_loss, grad_embed)


def solution(mesh):
    in_specs = (P(("vocab", "batch"), None), P("vocab", None), P("vocab"), P(), P(), P())
    out_specs = (P(("vocab", "batch")), P(("vocab", "batch"), None))

    def step(hidden, *rest):
        group_tokens = hidden.shape[0] * lax.axis_size("vocab")
        chosen = fused_body if 2 * group_tokens == LANES else body
        return chosen(hidden, *rest)

    return jax.shard_map(
        step, mesh=mesh, in_specs=in_specs, out_specs=out_specs, check_vma=False
    )
```

profile of v0, /device:TPU:0, one launch (start us, length us, event | category | flops | bytes accessed | tf_op | source)
XLA Modules:
  0.0 33.7 jit_solution(14052524501584258467)
XLA Ops:
  0.6 0.7 %broadcast_in_dim.2 = bf16[8,8,1024]{2,1,0:T(8,128)(2,1)S(1)} broadcast(bf16[8,1024]{1,0:T(8,128)(2,1)} %param.6), dimensions={1,2} | broadcast | bytes 147456 | tf_op jit(solution)/shard_map/broadcast_in_dim | solution.py:222
  1.4 12.6 %all_to_all.10 = bf16[8,8,1024]{2,1,0:T(8,128)(2,1)S(1)} all-to-all(bf16[8,8,1024]{2,1,0:T(8,128)(2,1)S(1)} %broadcast_in_dim.2), channel_id=1, replica_groups={{12,20,8,16,4,28,0,24},{13,21,9,17,5,29,1,25},{14,22,10,18,6,30,2,26},{..., dimensions={0} | all-to-all | bytes 262144 | tf_op jit(solution)/shard_map/all_to_all | solution.py:223
  14.0 1.5 %collective-permute-start.1 = (bf16[64,1024]{1,0:T(8,128)(2,1)S(1)}, bf16[64,1024]{1,0:T(8,128)(2,1)S(1)}, u32[]{:S(2)}, u32[]{:S(2)}) collective-permute-start(bf16[64,1024]{1,0:T(8,128)(2,1)S(1)} %bitcast.4), channel_id=1, source_target_pairs={{0,2},{1,3},{2,0},{3,1},{4,6},{5,7},{6,4},{7,5},{8,10},{9,11},{10,... | collective-permute-start | bytes 393224 | tf_op jit(solution)/shard_map/ppermute | solution.py:272
  15.5 0.0 collective-permute-start
  15.5 3.4 %collective-permute-done.1.refs_2_ = bf16[64,1024]{1,0:T(8,128)(2,1)S(1)} collective-permute-done((bf16[64,1024]{1,0:T(8,128)(2,1)S(1)}, bf16[64,1024]{1,0:T(8,128)(2,1)S(1)}, u32[]{:S(2)}, u32[]{:S(2)}) %collective-permute-start.1) | collective-permute-done | bytes 131104 | tf_op jit(solution)/shard_map/ppermute | solution.py:272
  19.0 0.0 collective-permute-start.2
  19.0 1.7 %prepare.1 = (f32[8,256]{1,0:T(8,128)S(1)}, s32[1,256]{1,0:T(1,128)S(1)}, bf16[1024,1024]{1,0:T(8,128)(2,1)S(1)}) custom-call(s32[4]{0:T(128)} %sent_hbm.1, s32[8]{0:T(128)} %count_hbm.1, s32[64,200]{1,0:T(8,128)} %bitcast.8, s32[1,256]{1,0:T(1,128)} %bitcast.9, bf16[1024,1024]{1,0:T(8,128)(2,1)} %emb_hbm.1), custom_call_target="tpu_custom_call" | custom-call | flops 65536 | bytes 4194304 | tf_op jit(solution)/shard_map/prepare/pallas_call | solution.py:226
  20.7 1.4 %stats.1 = f32[32,2,128]{2,1,0:T(2,128)} custom-call(f32[8,256]{1,0:T(8,128)S(1)} %get-tuple-element.9.bias_ref, s32[1,256]{1,0:T(1,128)S(1)} %get-tuple-element.10.target_ref, bf16[1024,1024]{1,0:T(8,128)(2,1)S(1)} %get-tuple-element.11.emb_ref, bf16[64,1024]{1,0:T(8,128)(2,1)S(1)} %bitcast.6), custom_call_target="tpu_custom_call" | custom-call | flops 134217728 | bytes 2097152 | tf_op jit(solution)/shard_map/stats/pallas_call | solution.py:253
  22.1 3.1 %all-to-all-start.1 = ((f32[32,2,128]{2,1,0:T(2,128)}), f32[32,2,128]{2,1,0:T(2,128)S(1)}, u32[]{:S(2)}, u32[]{:S(2)}) async-start(f32[32,2,128]{2,1,0:T(2,128)} %stats.1), calls=%async_computation.1 | async-start | bytes 65536 | tf_op jit(solution)/shard_map/all_to_all | solution.py:267
  25.2 0.0 collective-permute-done.refs_1_
  25.2 0.0 collective-permute-done.2.refs_3_
  25.2 0.3 %scores.1 = (f32[256,256]{1,0:T(8,128)S(1)}, bf16[256,1024]{1,0:T(8,128)(2,1)S(1)}) custom-call(f32[8,256]{1,0:T(8,128)S(1)} %get-tuple-element.9.bias_ref, s32[1,256]{1,0:T(1,128)S(1)} %get-tuple-element.10.target_ref, bf16[1024,1024]{1,0:T(8,128)(2,1)S(1)} %get-tuple-element.11.emb_ref, bf16[64,1024]{1,0:T(8,128)(2,1)S(1)} %bitcast.7, ...), custom_call_target="tpu_custom_call" | custom-call | flops 134217728 | bytes 524288 | tf_op jit(solution)/shard_map/scores/pallas_call | solution.py:275
  25.6 6.9 %all-to-all-done.1.stats_ref = f32[32,2,128]{2,1,0:T(2,128)S(1)} async-done(((f32[32,2,128]{2,1,0:T(2,128)}), f32[32,2,128]{2,1,0:T(2,128)S(1)}, u32[]{:S(2)}, u32[]{:S(2)}) %all-to-all-start.1) | async-done | bytes 32800 | tf_op jit(solution)/shard_map/all_to_all | solution.py:267
  32.5 1.2 %grad.1 = (f32[1,8]{1,0:T(1,128)}, bf16[256,1024]{1,0:T(8,128)(2,1)}) custom-call(f32[32,2,128]{2,1,0:T(2,128)S(1)} %all-to-all-done.1.stats_ref, s32[1,256]{1,0:T(1,128)S(1)} %get-tuple-element.10.target_ref, f32[256,256]{1,0:T(8,128)S(1)} %get-tuple-element.12.logits_ref, bf16[256,1024]{1,0:T(8,128)(2,1)S(1)} %get-tuple-element.13.everyone_ref), custom_call_target="tpu_custom_call" | custom-call | flops 134217728 | bytes 524288 | tf_op jit(solution)/shard_map/grad/pallas_call | solution.py:291
Async XLA Ops:
  14.0 5.0 %collective-permute-start.1 = (bf16[64,1024]{1,0:T(8,128)(2,1)S(1)}, bf16[64,1024]{1,0:T(8,128)(2,1)S(1)}, u32[]{:S(2)}, u32[]{:S(2)}) collective-permute-start(bf16[64,1024]{1,0:T(8,128)(2,1)S(1)} %bitcast.4), channel_id=1, source_target_pairs={{0,2},{1,3},{2,0},{3,1},{4,6},{5,7},{6,4},{7,5},{8,10},{9,11},{10,... | collective-permute-start | bytes 393224 | tf_op jit(solution)/shard_map/ppermute | solution.py:272
  15.5 9.7 %collective-permute-start = (bf16[64,1024]{1,0:T(8,128)(2,1)S(1)}, bf16[64,1024]{1,0:T(8,128)(2,1)S(1)}, u32[]{:S(2)}, u32[]{:S(2)}) collective-permute-start(bf16[64,1024]{1,0:T(8,128)(2,1)S(1)} %bitcast.5), channel_id=1, source_target_pairs={{0,1},{1,0},{2,3},{3,2},{4,5},{5,4},{6,7},{7,6},{8,9},{9,8},{10,11... | collective-permute-start | bytes 393224 | tf_op jit(solution)/shard_map/ppermute | solution.py:272
  19.0 6.3 %collective-permute-start.2 = (bf16[64,1024]{1,0:T(8,128)(2,1)S(1)}, bf16[64,1024]{1,0:T(8,128)(2,1)S(1)}, u32[]{:S(2)}, u32[]{:S(2)}) collective-permute-start(bf16[64,1024]{1,0:T(8,128)(2,1)S(1)} %collective-permute-done.1.refs_2_), channel_id=1, source_target_pairs={{0,1},{1,0},{2,3},{3,2},{4,5},{5,4},{6,7},{7,6},{8,9},{9,8},{10,11... | collective-permute-start | bytes 393224 | tf_op jit(solution)/shard_map/ppermute | solution.py:272
  22.1 10.4 %all-to-all-start.1 = ((f32[32,2,128]{2,1,0:T(2,128)}), f32[32,2,128]{2,1,0:T(2,128)S(1)}, u32[]{:S(2)}, u32[]{:S(2)}) async-start(f32[32,2,128]{2,1,0:T(2,128)} %stats.1), calls=%async_computation.1 | async-start | bytes 65536 | tf_op jit(solution)/shard_map/all_to_all | solution.py:267
where the time goes:
time: 34 us; the launch traced here: 33.7 us
  blocking collectives  12.6 us (37%)
  waiting for transfers between devices  10.3 us (30%)
  Pallas kernels  4.7 us (14%)
  starting transfers between devices  4.63 us (14%)
  local copies, waits for them, and re-layouts  0.73 us (2%)
  between operations  0.68 us (2%)
    all_to_all x1, blocking collectives, fused_body(): lax.all_to_all(copies, both, 0, 0, tiled=True, axis_index_groups=groups)  12.6 us
    all_to_all x1, waiting for transfers between devices, fused_body(): stats = lax.all_to_all(stats, both, 0, 0, tiled=True)  6.88 us
    ppermute x3, waiting for transfers between devices, fused_body(): received = [lax.ppermute(piece, 'batch', pairs) for piece in pieces]  3.45 us
    all_to_all x1, starting transfers between devices, fused_body(): stats = lax.all_to_all(stats, both, 0, 0, tiled=True)  3.1 us
    pallas_call x1, Pallas kernels, fused_body(): pl.pallas_call(functools.partial(prepare_kernel, order, tok_dev, batch_co...  1.69 us
    ppermute x3, starting transfers between devices, fused_body(): received = [lax.ppermute(piece, 'batch', pairs) for piece in pieces]  1.52 us
    pallas_call x1, Pallas kernels, fused_body(): pl.pallas_call(stats_kernel, out_shape=struct((devices, 2, 2 * group_toke...  1.45 us
    pallas_call x1, Pallas kernels, fused_body(): pl.pallas_call(functools.partial(grad_kernel, order, tok_dev, batch_count...  1.22 us
  transfers between devices with their start and end apart: 4, of which 2 were waited for; matrix products, arithmetic and copies ran while one was open for 0% of the time, Pallas kernels for 10%

commit v1 on v0

--- a/solution.py
+++ b/solution.py
@@ -18,6 +18,10 @@
 
 def centre_first(count):
     return sorted(range(count), key=lambda i: (abs(2 * (i // 2) - count // 2 + 1), -(i % 2), i))
+
+
+def twist(place, count):
+    return place // (count // 2)
 
 
 def iota(shape, axis):
@@ -44,14 +48,16 @@
     batch_index = lax.axis_index("batch")
     local_blocks, tokens = bias_ref.shape
     group_tokens = tokens // batch_count
+    vocab_count = group_tokens // tok_dev
     languages = lists_ref.shape[1]
 
     lane = iota((1, tokens), 1)
-    source = batch_index ^ (lane // group_tokens)
     position = (lane % group_tokens) // tok_dev
     place = jnp.zeros((1, tokens), jnp.int32)
     for j, v in enumerate(order):
         place = jnp.where(position == j, v, place)
+    twists = twist(place, vocab_count) ^ twist(vocab_index, vocab_count)
+    source = batch_index ^ (lane // group_tokens) ^ twists
     token = (place * batch_count + source) * tok_dev + lane % tok_dev
     sentence = token // SEQ
 
@@ -154,15 +160,22 @@
 
     rows = []
     for m in range(batch_count):
-        group = batch_index ^ m
-        parts = stats_ref[pl.ds(group, vocab_count, stride=batch_count), 0, :]
-        peak = jnp.max(parts, axis=0, keepdims=True)
-        totals = pltpu.roll(parts, group_tokens, 1)
-        total = jnp.sum(totals * jnp.exp(parts - peak), axis=0, keepdims=True)
+        group = batch_index ^ twist(vocab_index, vocab_count) ^ m
+        half = vocab_count // 2
+        starts = (group, half * batch_count + (group ^ 1))
+        halves = [stats_ref[pl.ds(start, half, stride=batch_count), 0, :] for start in starts]
+        peaks = [jnp.max(parts, axis=0, keepdims=True) for parts in halves]
+        peak = jnp.maximum(*peaks)
+        total = jnp.zeros_like(peak)
+        for parts in halves:
+            totals = pltpu.roll(parts, group_tokens, 1)
+            total = total + jnp.sum(totals * jnp.exp(parts - peak), axis=0, keepdims=True)
         log_total = peak + jnp.log(total)
         if m == 0:
-            aimed = stats_ref[pl.ds(group, vocab_count, stride=batch_count), 1, :]
-            loss = log_total - jnp.sum(aimed, axis=0, keepdims=True)
+            loss = log_total
+            for start in starts:
+                aimed = stats_ref[pl.ds(start, half, stride=batch_count), 1, :]
+                loss = loss - jnp.sum(aimed, axis=0, keepdims=True)
             my_place = jnp.int32(0)
             for j, v in enumerate(order):
                 my_place = jnp.where(vocab_index == v, j, my_place)
@@ -216,7 +229,9 @@
     devices = vocab_count * batch_count
     order = centre_first(vocab_count)
     both = ("vocab", "batch")
-    groups = [[v * batch_count + b for v in order] for b in range(batch_count)]
+    groups = [
+        [v * batch_count + (b ^ twist(v, vocab_count)) for v in order] for b in range(batch_count)
+    ]
     struct = jax.ShapeDtypeStruct
 
     copies = jnp.broadcast_to(hidden[None], (vocab_count, tok_dev, width))

time: 34 us -> 34.2 us (level)
  blocking collectives: 12.6 us -> 11.5 us
  waiting for transfers between devices: 10.3 us -> 11.1 us
  starting transfers between devices: 4.63 us -> 5.27 us
    all_to_all x1, blocking collectives: 12.6 us -> 11.5 us  [fused_body(): lax.all_to_all(copies, both, 0, 0, tiled=True, axis_index_groups=groups)]
    ppermute x3, waiting for transfers between devices: 3.45 us -> 4.17 us  [fused_body(): received = [lax.ppermute(piece, 'batch', pairs) for piece in pieces]]
    ppermute x3, starting transfers between devices: 1.52 us -> 2.09 us  [fused_body(): received = [lax.ppermute(piece, 'batch', pairs) for piece in pieces]]
where the time goes in v1:
time: 34.2 us; the launch traced here: 33.9 us
  blocking collectives  11.5 us (34%)
  waiting for transfers between devices  11.1 us (32%)
  starting transfers between devices  5.27 us (15%)
  Pallas kernels  4.69 us (14%)
  local copies, waits for them, and re-layouts  0.73 us (2%)
  between operations  0.68 us (2%)
    all_to_all x1, blocking collectives, fused_body(): lax.all_to_all(copies, both, 0, 0, tiled=True, axis_index_groups=groups)  11.5 us
    all_to_all x1, waiting for transfers between devices, fused_body(): stats = lax.all_to_all(stats, both, 0, 0, tiled=True)  6.89 us
    ppermute x3, waiting for transfers between devices, fused_body(): received = [lax.ppermute(piece, 'batch', pairs) for piece in pieces]  4.17 us
    all_to_all x1, starting transfers between devices, fused_body(): stats = lax.all_to_all(stats, both, 0, 0, tiled=True)  3.17 us
    ppermute x3, starting transfers between devices, fused_body(): received = [lax.ppermute(piece, 'batch', pairs) for piece in pieces]  2.09 us
    pallas_call x1, Pallas kernels, fused_body(): pl.pallas_call(functools.partial(prepare_kernel, order, tok_dev, batch_co...  1.69 us
    pallas_call x1, Pallas kernels, fused_body(): pl.pallas_call(stats_kernel, out_shape=struct((devices, 2, 2 * group_toke...  1.45 us
    pallas_call x1, Pallas kernels, fused_body(): pl.pallas_call(functools.partial(grad_kernel, order, tok_dev, batch_count...  1.21 us
  transfers between devices with their start and end apart: 4, of which 2 were waited for; matrix products, arithmetic and copies ran while one was open for 0% of the time, Pallas kernels for 10%

profile of v1, /device:TPU:0, one launch (start us, length us, event | category | flops | bytes accessed | tf_op | source)
XLA Modules:
  0.0 33.9 jit_solution(15785138408041671254)
XLA Ops:
  0.6 0.7 %broadcast_in_dim.2 = bf16[8,8,1024]{2,1,0:T(8,128)(2,1)S(1)} broadcast(bf16[8,1024]{1,0:T(8,128)(2,1)} %param.6), dimensions={1,2} | broadcast | bytes 147456 | tf_op jit(solution)/shard_map/broadcast_in_dim | solution.py:237
  1.4 11.5 %all_to_all.10 = bf16[8,8,1024]{2,1,0:T(8,128)(2,1)S(1)} all-to-all(bf16[8,8,1024]{2,1,0:T(8,128)(2,1)S(1)} %broadcast_in_dim.2), channel_id=1, replica_groups={{12,21,8,17,4,29,0,25},{13,20,9,16,5,28,1,24},{14,23,10,19,6,31,2,27},{..., dimensions={0} | all-to-all | bytes 262144 | tf_op jit(solution)/shard_map/all_to_all | solution.py:238
  12.9 1.5 %collective-permute-start.1 = (bf16[64,1024]{1,0:T(8,128)(2,1)S(1)}, bf16[64,1024]{1,0:T(8,128)(2,1)S(1)}, u32[]{:S(2)}, u32[]{:S(2)}) collective-permute-start(bf16[64,1024]{1,0:T(8,128)(2,1)S(1)} %bitcast.4), channel_id=1, source_target_pairs={{0,2},{1,3},{2,0},{3,1},{4,6},{5,7},{6,4},{7,5},{8,10},{9,11},{10,... | collective-permute-start | bytes 393224 | tf_op jit(solution)/shard_map/ppermute | solution.py:287
  14.4 0.6 %collective-permute-start = (bf16[64,1024]{1,0:T(8,128)(2,1)S(1)}, bf16[64,1024]{1,0:T(8,128)(2,1)S(1)}, u32[]{:S(2)}, u32[]{:S(2)}) collective-permute-start(bf16[64,1024]{1,0:T(8,128)(2,1)S(1)} %bitcast.5), channel_id=1, source_target_pairs={{0,1},{1,0},{2,3},{3,2},{4,5},{5,4},{6,7},{7,6},{8,9},{9,8},{10,11... | collective-permute-start | bytes 393224 | tf_op jit(solution)/shard_map/ppermute | solution.py:287
  15.0 4.2 %collective-permute-done.1.refs_2_ = bf16[64,1024]{1,0:T(8,128)(2,1)S(1)} collective-permute-done((bf16[64,1024]{1,0:T(8,128)(2,1)S(1)}, bf16[64,1024]{1,0:T(8,128)(2,1)S(1)}, u32[]{:S(2)}, u32[]{:S(2)}) %collective-permute-start.1) | collective-permute-done | bytes 131104 | tf_op jit(solution)/shard_map/ppermute | solution.py:287
  19.1 0.0 collective-permute-start.2
  19.1 1.7 %prepare.1 = (f32[8,256]{1,0:T(8,128)S(1)}, s32[1,256]{1,0:T(1,128)S(1)}, bf16[1024,1024]{1,0:T(8,128)(2,1)S(1)}) custom-call(s32[4]{0:T(128)} %sent_hbm.1, s32[8]{0:T(128)} %count_hbm.1, s32[64,200]{1,0:T(8,128)} %bitcast.8, s32[1,256]{1,0:T(1,128)} %bitcast.9, bf16[1024,1024]{1,0:T(8,128)(2,1)} %emb_hbm.1), custom_call_target="tpu_custom_call" | custom-call | flops 65536 | bytes 4194304 | tf_op jit(solution)/shard_map/prepare/pallas_call | solution.py:241
  20.8 1.4 %stats.1 = f32[32,2,128]{2,1,0:T(2,128)} custom-call(f32[8,256]{1,0:T(8,128)S(1)} %get-tuple-element.9.bias_ref, s32[1,256]{1,0:T(1,128)S(1)} %get-tuple-element.10.target_ref, bf16[1024,1024]{1,0:T(8,128)(2,1)S(1)} %get-tuple-element.11.emb_ref, bf16[64,1024]{1,0:T(8,128)(2,1)S(1)} %bitcast.6), custom_call_target="tpu_custom_call" | custom-call | flops 134217728 | bytes 2097152 | tf_op jit(solution)/shard_map/stats/pallas_call | solution.py:268
  22.3 3.2 %all-to-all-start.1 = ((f32[32,2,128]{2,1,0:T(2,128)}), f32[32,2,128]{2,1,0:T(2,128)S(1)}, u32[]{:S(2)}, u32[]{:S(2)}) async-start(f32[32,2,128]{2,1,0:T(2,128)} %stats.1), calls=%async_computation.1 | async-start | bytes 65536 | tf_op jit(solution)/shard_map/all_to_all | solution.py:282
  25.5 0.0 collective-permute-done.refs_1_
  25.5 0.0 collective-permute-done.2.refs_3_
  25.5 0.3 %scores.1 = (f32[256,256]{1,0:T(8,128)S(1)}, bf16[256,1024]{1,0:T(8,128)(2,1)S(1)}) custom-call(f32[8,256]{1,0:T(8,128)S(1)} %get-tuple-element.9.bias_ref, s32[1,256]{1,0:T(1,128)S(1)} %get-tuple-element.10.target_ref, bf16[1024,1024]{1,0:T(8,128)(2,1)S(1)} %get-tuple-element.11.emb_ref, bf16[64,1024]{1,0:T(8,128)(2,1)S(1)} %bitcast.7, ...), custom_call_target="tpu_custom_call" | custom-call | flops 134217728 | bytes 524288 | tf_op jit(solution)/shard_map/scores/pallas_call | solution.py:290
  25.8 6.9 %all-to-all-done.1.stats_ref = f32[32,2,128]{2,1,0:T(2,128)S(1)} async-done(((f32[32,2,128]{2,1,0:T(2,128)}), f32[32,2,128]{2,1,0:T(2,128)S(1)}, u32[]{:S(2)}, u32[]{:S(2)}) %all-to-all-start.1) | async-done | bytes 32800 | tf_op jit(solution)/shard_map/all_to_all | solution.py:282
  32.7 1.2 %grad.1 = (f32[1,8]{1,0:T(1,128)}, bf16[256,1024]{1,0:T(8,128)(2,1)}) custom-call(f32[32,2,128]{2,1,0:T(2,128)S(1)} %all-to-all-done.1.stats_ref, s32[1,256]{1,0:T(1,128)S(1)} %get-tuple-element.10.target_ref, f32[256,256]{1,0:T(8,128)S(1)} %get-tuple-element.12.logits_ref, bf16[256,1024]{1,0:T(8,128)(2,1)S(1)} %get-tuple-element.13.everyone_ref), custom_call_target="tpu_custom_call" | custom-call | flops 134217728 | bytes 524288 | tf_op jit(solution)/shard_map/grad/pallas_call | solution.py:306
Async XLA Ops:
  12.9 6.3 %collective-permute-start.1 = (bf16[64,1024]{1,0:T(8,128)(2,1)S(1)}, bf16[64,1024]{1,0:T(8,128)(2,1)S(1)}, u32[]{:S(2)}, u32[]{:S(2)}) collective-permute-start(bf16[64,1024]{1,0:T(8,128)(2,1)S(1)} %bitcast.4), channel_id=1, source_target_pairs={{0,2},{1,3},{2,0},{3,1},{4,6},{5,7},{6,4},{7,5},{8,10},{9,11},{10,... | collective-permute-start | bytes 393224 | tf_op jit(solution)/shard_map/ppermute | solution.py:287
  14.4 11.1 %collective-permute-start = (bf16[64,1024]{1,0:T(8,128)(2,1)S(1)}, bf16[64,1024]{1,0:T(8,128)(2,1)S(1)}, u32[]{:S(2)}, u32[]{:S(2)}) collective-permute-start(bf16[64,1024]{1,0:T(8,128)(2,1)S(1)} %bitcast.5), channel_id=1, source_target_pairs={{0,1},{1,0},{2,3},{3,2},{4,5},{5,4},{6,7},{7,6},{8,9},{9,8},{10,11... | collective-permute-start | bytes 393224 | tf_op jit(solution)/shard_map/ppermute | solution.py:287
  19.1 6.3 %collective-permute-start.2 = (bf16[64,1024]{1,0:T(8,128)(2,1)S(1)}, bf16[64,1024]{1,0:T(8,128)(2,1)S(1)}, u32[]{:S(2)}, u32[]{:S(2)}) collective-permute-start(bf16[64,1024]{1,0:T(8,128)(2,1)S(1)} %collective-permute-done.1.refs_2_), channel_id=1, source_target_pairs={{0,1},{1,0},{2,3},{3,2},{4,5},{5,4},{6,7},{7,6},{8,9},{9,8},{10,11... | collective-permute-start | bytes 393224 | tf_op jit(solution)/shard_map/ppermute | solution.py:287
  22.3 10.4 %all-to-all-start.1 = ((f32[32,2,128]{2,1,0:T(2,128)}), f32[32,2,128]{2,1,0:T(2,128)S(1)}, u32[]{:S(2)}, u32[]{:S(2)}) async-start(f32[32,2,128]{2,1,0:T(2,128)} %stats.1), calls=%async_computation.1 | async-start | bytes 65536 | tf_op jit(solution)/shard_map/all_to_all | solution.py:282
